TPU v7x, 32 devices: a whole 2x2x4 slice. The times are simulated.
32 devices in a mesh: dp: 2 (over x), row: 4 (over z), col: 4 (over y, core).
Axes of the slice: x: 2, y: 2, z: 4, core: 2. Of those that a mesh axis runs over, the one named last changes fastest.
Arguments:
- stash_codes: int32 [1024, 4096], P(('dp', 'col'), 'row'), may hold values from 0 to 3
- stash_scales: int32 [1024, 32], P(('dp', 'col'), 'row'), may hold values from 1 to 8
- pad_mask: int32 [1024], P(('dp', 'col')), may hold values 0 or 1
- cotangent: bfloat16 [1024, 4096], P(('dp', 'col'), 'row'), may hold values from -3 to 3
- w_gate: bfloat16 [4096, 10240], P('row', 'col'), may hold values from -0.09375 to 0.09375
- w_up: bfloat16 [4096, 10240], P('row', 'col'), may hold values from -0.09375 to 0.09375
- w_out: bfloat16 [4096, 10240], P('row', 'col'), may hold values from -0.09375 to 0.09375
Outputs:
- input_grad: float32 [1024, 4096], P(('dp', 'col'), 'row')
- gate_weight_grad: float32 [4096, 10240], P('row', 'col')
- up_weight_grad: float32 [4096, 10240], P('row', 'col')
- out_weight_grad: float32 [4096, 10240], P('row', 'col')
All inputs are finite; a program needn't handle non-finite values. No bound on the sum of `pad_mask` on one device may be relied on, other than what follows from the above.
Results may differ from a plain program's by a relative error of at most 0.0029.
Values may be sent and summed in bfloat16 or wider, within the bound.
No kernel may reach another device: no remote copies, remote signals or barrier semaphores. Data moves between devices by JAX's collectives and lax.ppermute only.
A program may use at most 192 MiB of HBM per device.

v0:
```python
import jax
import jax.numpy as jnp
from jax import lax
from jax.sharding import PartitionSpec as P

root_term = 0.7978845608028654
cubic_term = 0.044715


def gelu_pair(values):
    inside = root_term * (values + cubic_term * values * values * values)
    tangent = jnp.tanh(inside)
    activated = 0.5 * values * (1.0 + tangent)
    derivative = 0.5 * (1.0 + tangent) + 0.5 * values * (1.0 - tangent * tangent) * root_term * (
        1.0 + 3.0 * cubic_term * values * values
    )
    return (activated, derivative)


def unpack_stash(stash_codes, stash_scales):
    blocks = stash_scales.shape[1]
    block_width = stash_codes.shape[1] // blocks
    levels = (
        (2 * stash_codes - 3).astype(jnp.float32).reshape(stash_codes.shape[0], blocks, block_width)
    )
    scaled = levels * stash_scales.astype(jnp.float32)[:, :, None] / 16.0
    return scaled.reshape(stash_codes.shape).astype(jnp.bfloat16)


def per_device(stash_codes, stash_scales, pad_mask, cotangent, w_gate, w_up, w_out):
    stashed = unpack_stash(stash_codes, stash_scales)
    live_grad = (cotangent.astype(jnp.float32) * pad_mask.astype(jnp.float32)[:, None]).astype(
        jnp.bfloat16
    )
    stash_all, grad_all = (
        lax.all_gather(stashed, "col", axis=0, tiled=True),
        lax.all_gather(live_grad, "col", axis=0, tiled=True),
    )
    ff_local = w_gate.shape[1]
    joined = lax.psum_scatter(
        jnp.concatenate(
            [
                jnp.dot(stash_all, w_gate, preferred_element_type=jnp.float32),
                jnp.dot(stash_all, w_up, preferred_element_type=jnp.float32),
                jnp.dot(grad_all, w_out, preferred_element_type=jnp.float32),
            ],
            axis=1,
        ),
        "row",
        scatter_dimension=0,
        tiled=True,
    )
    gate_pre = joined[:, :ff_local]
    up_part = joined[:, ff_local : 2 * ff_local]
    back_grad = joined[:, 2 * ff_local :]
    activated, derivative = gelu_pair(gate_pre)
    hidden = (activated * up_part).astype(jnp.bfloat16)
    gate_grad = (back_grad * up_part * derivative).astype(jnp.bfloat16)
    up_grad = (back_grad * activated).astype(jnp.bfloat16)
    local_stack = jnp.concatenate([gate_grad, up_grad, hidden], axis=1)
    stacked = lax.all_gather(local_stack, "row", axis=0, tiled=True)
    transposed = (((1,), (1,)), ((), ()))
    gate_rows = stacked[:, :ff_local]
    up_rows = stacked[:, ff_local : 2 * ff_local]
    input_grad = lax.psum_scatter(
        lax.dot_general(gate_rows, w_gate, transposed, preferred_element_type=jnp.float32)
        + lax.dot_general(up_rows, w_up, transposed, preferred_element_type=jnp.float32),
        "col",
        scatter_dimension=0,
        tiled=True,
    )
    contract = (((0,), (0,)), ((), ()))
    inputs_part = lax.dot_general(
        stash_all, stacked[:, : 2 * ff_local], contract, preferred_element_type=jnp.float32
    )
    second = lax.dot_general(
        grad_all, stacked[:, 2 * ff_local :], contract, preferred_element_type=jnp.float32
    )
    summed = lax.psum(jnp.concatenate([inputs_part, second], axis=1), "dp")
    return (
        input_grad,
        summed[:, :ff_local],
        summed[:, ff_local : 2 * ff_local],
        summed[:, 2 * ff_local :],
    )


def solution(mesh):
    return jax.shard_map(
        per_device,
        mesh=mesh,
        in_specs=(
            P(("dp", "col"), "row"),
            P(("dp", "col"), "row"),
            P(("dp", "col")),
            P(("dp", "col"), "row"),
            P("row", "col"),
            P("row", "col"),
            P("row", "col"),
        ),
        out_specs=(P(("dp", "col"), "row"), P("row", "col"), P("row", "col"), P("row", "col")),
        check_vma=False,
    )
```

profile of v0, /device:TPU:0, one launch (start us, length us, event | category | flops | bytes accessed | tf_op | source)
XLA Modules:
  0.0 1232.1 jit_solution(16199917067725401654)
XLA Ops:
  7.2 0.7 convert_element_type.28
  8.2 1.9 fusion.19
  10.2 0.7 convert_element_type.31
  10.9 1.8 multiply_convert_fusion.2
  12.7 17.0 %all-gather.4.cloned.1.call-done = bf16[512,1024]{1,0:T(8,128)(2,1)} async-done(((bf16[128,1024]{1,0:T(8,128)(2,1)}), bf16[512,1024]{1,0:T(8,128)(2,1)}) %all-gather.4.cloned.1.call-update) | async-done | bytes 1048592 | tf_op jit(solution)/shard_map/all_gather | solution.py:36
  29.7 8.1 fusion.22
  37.9 7.3 fusion.21
  45.1 3.5 all-gather.6.cloned.1.call-done
  48.6 5.2 fusion.23
  53.9 0.7 copy-done.1
  54.5 5.8 pad_maximum_fusion.1
  60.4 262.7 %reduce-scatter.3.cloned.1.call-done = f32[128,7680]{1,0:T(8,128)} async-done(((f32[512,7680]{1,0:T(8,128)}), f32[128,7680]{1,0:T(8,128)}) %reduce-scatter.3.cloned.1.call-update) | async-done | bytes 3932176 | tf_op jit(solution)/shard_map/reduce_scatter | solution.py:40
  323.1 3.2 fusion.17
  326.3 1.4 pad_maximum_fusion.2
  327.8 142.2 %all-gather.8.cloned.1.call-done = bf16[512,7680]{1,0:T(8,128)(2,1)} async-done(((bf16[128,7680]{1,0:T(8,128)(2,1)}), bf16[512,7680]{1,0:T(8,128)(2,1)}) %all-gather.8.cloned.1.call-update) | async-done | bytes 7864336 | tf_op jit(solution)/shard_map/all_gather | solution.py:61
  469.9 7.4 fusion.2
  477.3 7.6 fusion
  485.0 14.9 %pad_maximum_fusion = f32[1024,7680]{1,0:T(8,128)} fusion(f32[1024,2560]{1,0:T(8,128)} %fusion.2, f32[1024,5120]{1,0:T(8,128)S(1)} %fusion), kind=kLoop, calls=%fused_computation | loop fusion | flops 7864320 | bytes 62914560 | tf_op jit(solution)/shard_map/concatenate | solution.py:79
  499.9 0.2 reduce-scatter.5.cloned.1.call-start
  500.1 5.7 fusion.4
  505.8 7.5 fusion.8
  513.4 677.7 %all-reduce.2.cloned.1.call-done = f32[1024,7680]{1,0:T(8,128)} async-done(((f32[1024,7680]{1,0:T(8,128)}), f32[1024,7680]{1,0:T(8,128)}) %all-reduce.2.cloned.1.call-update) | async-done | bytes 31457296 | tf_op jit(solution)/shard_map/psum | solution.py:79
  1191.0 22.7 %fusion.20 = (f32[1024,2560]{1,0:T(8,128)}, f32[1024,2560]{1,0:T(8,128)}, f32[1024,2560]{1,0:T(8,128)}) fusion(f32[1024,7680]{1,0:T(8,128)} %all-reduce.2.cloned.1.call-done), kind=kLoop, calls=%fused_computation.28 | loop fusion | bytes 62914560 | tf_op jit(solution)/shard_map/slice | solution.py:84
  1213.7 11.5 reduce-scatter.5.cloned.1.call-done
  (20 shorter events, 0.6 us)
Async XLA Ops:
  7.2 22.6 %all-gather.4.cloned.1.call-start = ((), (), s32[]{:S(2)}) async-start(), calls=%async_computation.2 | async-start | bytes 1310720 | tf_op jit(solution)/shard_map/all_gather | solution.py:36
  10.1 38.4 %all-gather.6.cloned.1.call-start = ((), (), s32[]{:S(2)}) async-start(), calls=%async_computation.3 | async-start | bytes 1310720 | tf_op jit(solution)/shard_map/all_gather | solution.py:37
  12.6 310.5 %reduce-scatter.3.cloned.1.call-start = ((), (), s32[]{:S(2)}) async-start(), calls=%async_computation.4 | async-start | bytes 19660800 | tf_op jit(solution)/shard_map/reduce_scatter | solution.py:40
  29.7 8.1 copy-start.2
  48.6 5.3 copy-start
  48.6 5.9 copy-start.1
  60.3 409.6 %copy-start.3 = (bf16[512,1024]{1,0:T(8,128)(2,1)S(1)}, bf16[512,1024]{1,0:T(8,128)(2,1)}, u32[]{:S(2)}) copy-start(bf16[512,1024]{1,0:T(8,128)(2,1)} %all-gather.6.cloned.1.call-done) | copy-start | bytes 3145732
  60.3 409.6 %all-gather.8.cloned.1.call-start = ((), (), s32[]{:S(2)}) async-start(), calls=%async_computation.5 | async-start | bytes 9830400 | tf_op jit(solution)/shard_map/all_gather | solution.py:61
  327.7 863.3 %all-reduce.2.cloned.1.call-start = ((), (), s32[]{:S(2)}) async-start(), calls=%async_computation.7 | async-start | bytes 62914560 | tf_op jit(solution)/shard_map/psum | solution.py:79
  499.9 725.3 %reduce-scatter.5.cloned.1.call-start = ((), (), s32[]{:S(2)}) async-start(), calls=%async_computation.6 | async-start | bytes 2621440 | tf_op jit(solution)/shard_map/reduce_scatter | solution.py:65
Sparse Core Ops, SparseCore 0:
  10.3 19.4 all-gather.3
  31.9 16.6 all-gather.5
  60.4 262.6 reduce-scatter.2
  327.8 142.0 all-gather.7
  500.0 690.9 all-reduce.1
  1194.0 31.1 reduce-scatter.4
where the time goes:
time: 1230 us
  waiting for transfers between devices  1110 us (90%)
  matrix products  48.9 us (4%)
  other arithmetic  30.3 us (2%)
  local copies, waits for them, and re-layouts  23.6 us (2%)
  between operations  14.2 us (1%)
    psum x1, waiting for transfers between devices, per_device(): summed = lax.psum(jnp.concatenate([inputs_part, second], axis=1), 'dp')  678 us
    reduce_scatter x1, waiting for transfers between devices, per_device(): lax.psum_scatter(jnp.concatenate([jnp.dot(stash_all, w_gate, preferred_el...  263 us
    all_gather x1, waiting for transfers between devices, per_device(): stacked = lax.all_gather(local_stack, 'row', axis=0, tiled=True)  142 us
  transfers between devices with their start and end apart: 6, of which 6 were waited for; matrix products, arithmetic and copies ran while one was open for 4% of the time, Pallas kernels for 0%

commit v1 on v0

--- a/solution.py
+++ b/solution.py
@@ -76,7 +76,9 @@
     second = lax.dot_general(
         grad_all, stacked[:, 2 * ff_local :], contract, preferred_element_type=jnp.float32
     )
-    summed = lax.psum(jnp.concatenate([inputs_part, second], axis=1), "dp")
+    part = jnp.concatenate([inputs_part, second], axis=1)
+    parts = lax.all_gather(part, "dp")
+    summed = jnp.sum(parts, axis=0)
     return (
         input_grad,
         summed[:, :ff_local],

time: 1230 us -> 1280 us (1.041)
  other arithmetic: 30.3 us -> 64.3 us
  waiting for transfers between devices: 1110 us -> 1130 us
    all_gather x0 -> x1, waiting for transfers between devices: none -> 703 us  [per_device(): parts = lax.all_gather(part, 'dp')]
    psum x1 -> x0, waiting for transfers between devices: 678 us -> none  [per_device(): summed = lax.psum(jnp.concatenate([inputs_part, second], axis=1), 'dp')]
    reduce_sum x0 -> x1, other arithmetic: none -> 34 us  [per_device(): summed = jnp.sum(parts, axis=0)]
  transfers between devices with their start and end apart: 6 -> 6, of which waited for: 6 -> 5; matrix products, arithmetic and copies ran while one was open for 4% -> 7% of each run, Pallas kernels for 0% -> 0%
where the time goes in v1:
time: 1280 us
  waiting for transfers between devices  1130 us (88%)
  other arithmetic  64.3 us (5%)
  matrix products  51.8 us (4%)
  local copies, waits for them, and re-layouts  23.3 us (2%)
  between operations  14.2 us (1%)
    all_gather x1, waiting for transfers between devices, per_device(): parts = lax.all_gather(part, 'dp')  703 us
    reduce_scatter x1, waiting for transfers between devices, per_device(): lax.psum_scatter(jnp.concatenate([jnp.dot(stash_all, w_gate, preferred_el...  263 us
    all_gather x1, waiting for transfers between devices, per_device(): stacked = lax.all_gather(local_stack, 'row', axis=0, tiled=True)  142 us
    reduce_sum x1, other arithmetic, per_device(): summed = jnp.sum(parts, axis=0)  34 us
  transfers between devices with their start and end apart: 6, of which 5 were waited for; matrix products, arithmetic and copies ran while one was open for 7% of the time, Pallas kernels for 0%

profile of v1, /device:TPU:0, one launch (start us, length us, event | category | flops | bytes accessed | tf_op | source)
XLA Modules:
  0.0 1283.0 jit_solution(14442084789382581275)
XLA Ops:
  7.2 0.7 convert_element_type.28
  8.2 1.9 fusion.19
  10.2 0.7 convert_element_type.31
  10.9 1.8 multiply_convert_fusion.2
  12.7 17.0 %all-gather.6.cloned.1.call-done = bf16[512,1024]{1,0:T(8,128)(2,1)} async-done(((bf16[128,1024]{1,0:T(8,128)(2,1)}), bf16[512,1024]{1,0:T(8,128)(2,1)}) %all-gather.6.cloned.1.call-update) | async-done | bytes 1048592 | tf_op jit(solution)/shard_map/all_gather | solution.py:36
  29.7 8.1 fusion.22
  37.9 7.3 fusion.21
  45.1 3.5 all-gather.8.cloned.1.call-done
  48.6 5.2 fusion.23
  53.9 0.7 copy-done.1
  54.5 5.8 pad_maximum_fusion.1
  60.4 262.7 %reduce-scatter.3.cloned.1.call-done = f32[128,7680]{1,0:T(8,128)} async-done(((f32[512,7680]{1,0:T(8,128)}), f32[128,7680]{1,0:T(8,128)}) %reduce-scatter.3.cloned.1.call-update) | async-done | bytes 3932176 | tf_op jit(solution)/shard_map/reduce_scatter | solution.py:40
  323.1 3.2 fusion.17
  326.3 1.4 pad_maximum_fusion.2
  327.8 142.2 %all-gather.10.cloned.1.call-done = bf16[512,7680]{1,0:T(8,128)(2,1)} async-done(((bf16[128,7680]{1,0:T(8,128)(2,1)}), bf16[512,7680]{1,0:T(8,128)(2,1)}) %all-gather.10.cloned.1.call-update) | async-done | bytes 7864336 | tf_op jit(solution)/shard_map/all_gather | solution.py:61
  469.9 7.4 fusion.2
  477.3 7.6 fusion
  485.0 15.0 %pad_maximum_fusion = f32[1024,7680]{1,0:T(8,128)} fusion(f32[1024,2560]{1,0:T(8,128)} %fusion.2, f32[1024,5120]{1,0:T(8,128)S(1)} %fusion), kind=kLoop, calls=%fused_computation | loop fusion | flops 7864320 | bytes 62914560 | tf_op jit(solution)/shard_map/concatenate | solution.py:79
  499.9 0.2 reduce-scatter.5.cloned.1.call-start
  500.2 5.7 fusion.4
  505.9 10.5 fusion.8
  516.4 703.5 %all-gather.12.cloned.1.call-done = f32[2048,7680]{1,0:T(8,128)} async-done(((f32[1024,7680]{1,0:T(8,128)}), f32[2048,7680]{1,0:T(8,128)}) %all-gather.12.cloned.1.call-update) | async-done | bytes 62914576 | tf_op jit(solution)/shard_map/all_gather | solution.py:80
  1219.9 34.0 %reduce_sum.9 = f32[1024,7680]{1,0:T(8,128)} reduce(f32[2,1024,7680]{2,1,0:T(8,128)} %bitcast.18, f32[]{:T(128)} %constant.19.clone.1), dimensions={0}, to_apply=%region_2.0 | reduce | flops 7864320 | bytes 94371840 | tf_op jit(solution)/shard_map/reduce_sum | solution.py:81
  1253.8 22.3 %fusion.20 = (f32[1024,2560]{1,0:T(8,128)}, f32[1024,2560]{1,0:T(8,128)}, f32[1024,2560]{1,0:T(8,128)}) fusion(f32[1024,7680]{1,0:T(8,128)} %reduce_sum.9), kind=kLoop, calls=%fused_computation.28 | loop fusion | bytes 62914560 | tf_op jit(solution)/shard_map/slice | solution.py:86
  (21 shorter events, 0.6 us)
Async XLA Ops:
  7.2 22.6 %all-gather.6.cloned.1.call-start = ((), (), s32[]{:S(2)}) async-start(), calls=%async_computation.2 | async-start | bytes 1310720 | tf_op jit(solution)/shard_map/all_gather | solution.py:36
  10.1 38.4 %all-gather.8.cloned.1.call-start = ((), (), s32[]{:S(2)}) async-start(), calls=%async_computation.3 | async-start | bytes 1310720 | tf_op jit(solution)/shard_map/all_gather | solution.py:37
  12.6 310.5 %reduce-scatter.3.cloned.1.call-start = ((), (), s32[]{:S(2)}) async-start(), calls=%async_computation.4 | async-start | bytes 19660800 | tf_op jit(solution)/shard_map/reduce_scatter | solution.py:40
  29.7 8.1 copy-start.2
  48.6 5.3 copy-start
  48.6 5.9 copy-start.1
  60.3 409.6 %copy-start.3 = (bf16[512,1024]{1,0:T(8,128)(2,1)S(1)}, bf16[512,1024]{1,0:T(8,128)(2,1)}, u32[]{:S(2)}) copy-start(bf16[512,1024]{1,0:T(8,128)(2,1)} %all-gather.8.cloned.1.call-done) | copy-start | bytes 3145732
  60.3 409.6 %all-gather.10.cloned.1.call-start = ((), (), s32[]{:S(2)}) async-start(), calls=%async_computation.5 | async-start | bytes 9830400 | tf_op jit(solution)/shard_map/all_gather | solution.py:61
  327.7 892.1 %all-gather.12.cloned.1.call-start = ((), (), s32[]{:S(2)}) async-start(), calls=%async_computation.7 | async-start | bytes 94371840 | tf_op jit(solution)/shard_map/all_gather | solution.py:80
  499.9 776.2 %reduce-scatter.5.cloned.1.call-start = ((), (), s32[]{:S(2)}) async-start(), calls=%async_computation.6 | async-start | bytes 2621440 | tf_op jit(solution)/shard_map/reduce_scatter | solution.py:65
Sparse Core Ops, SparseCore 0:
  10.3 19.4 all-gather.5
  31.9 16.6 all-gather.7
  60.4 262.6 reduce-scatter.2
  327.8 142.0 all-gather.9
  500.1 719.7 all-gather.11
  1222.8 31.1 reduce-scatter.4
